TPU v7x, 512 devices: a whole 4x8x8 slice. The times are simulated.
512 devices in a mesh: node: 64 (over y_hi, z, x), head: 8 (over y_lo, core).
Axes of the slice: x: 4, y: 8 (y_hi: 2, y_lo: 4; y = y_hi * 4 + y_lo), z: 8, core: 2. Of those that a mesh axis runs over, the one named last changes fastest.
Arguments:
- features: bfloat16 [8192, 128], P('node'), may hold values from -1201 to 1201
- proj_weight: bfloat16 [128, 1024], P(None, 'head'), may hold values from -1 to 1
- score_source: float32 [8, 128], P('head'), may hold values from -1 to 1
- score_target: float32 [8, 128], P('head'), may hold values from -1 to 1
- out_weight: bfloat16 [1024, 256], P('head'), may hold values from -0.1875 to 0.1875
- presence: int32 [64, 64], P('node'), may hold values from 0 to 1, as said below
- tile_masks: int32 [64, 16, 128, 128], P('node'), may hold values 0 or 1
Outputs:
- mixed: bfloat16 [8192, 256], P('node')
Inputs may be any that keep to these rules, and one draw needn't show every extreme that they name: Each row holds exactly 16 ones; tile_masks[r, k] belongs to the k-th present tile of row r of presence, counted in ascending order of tile.
All inputs are finite; a program needn't handle non-finite values. No bound on the sum of `tile_masks` on one device may be relied on, other than what follows from the above.
Results may differ from a plain program's by a relative error of at most 0.015.
Values may be sent and summed in bfloat16 or wider, within the bound.
No kernel may reach another device: no remote copies, remote signals or barrier semaphores. Data moves between devices by JAX's collectives and lax.ppermute only.
A program may use at most 64 MiB of HBM per device.

v0:
```python
import math
import jax
import jax.numpy as jnp
from jax import lax
from jax.sharding import PartitionSpec as P


def leaky_relu(values):
    return jnp.where(values > 0, values, 0.2 * values)


def per_device(features, proj_weight, score_source, score_target, out_weight, presence, tile_masks):
    target_count = features.shape[0]
    heads_here = score_source.shape[0]
    head_width = score_source.shape[1]
    tile_width = tile_masks.shape[-1]
    row_tiles = presence.shape[0]

    def project(rows):
        return jnp.dot(rows, proj_weight, preferred_element_type=jnp.float32).astype(jnp.bfloat16)

    def head_terms(projected, vectors):
        widened = lax.optimization_barrier(projected).astype(jnp.float32)
        widened = widened.reshape(projected.shape[0], heads_here, head_width)
        return jnp.sum(widened * vectors[None], axis=-1).T

    local_proj = project(features)
    target_terms = head_terms(local_proj, score_target)
    first_row = lax.axis_index("node") * target_count
    target_ids = first_row + jnp.arange(target_count, dtype=jnp.int32)
    slots = jnp.maximum(jnp.cumsum(presence, axis=1) - 1, 0)
    tile_rows = jnp.arange(row_tiles, dtype=jnp.int32)

    def absorb(carry, block):
        running, denominator, accum = carry
        block_values, block_source, block_start = block
        span_rows = block_values.shape[0]
        column_ids = block_start + jnp.arange(span_rows, dtype=jnp.int32)
        column_tiles = column_ids // tile_width
        column_lanes = column_ids % tile_width
        present_here = jnp.take(presence, column_tiles, axis=1)
        slot_here = jnp.take(slots, column_tiles, axis=1)
        gathered = tile_masks[tile_rows[:, None], slot_here, :, column_lanes[None, :]]
        tile_bits = (
            (gathered * present_here[:, :, None])
            .transpose(0, 2, 1)
            .reshape(target_count, span_rows)
        )
        itself = column_ids[None, :] == target_ids[:, None]
        linked = (tile_bits == 1) & jnp.logical_not(itself) | itself
        edge_scores = leaky_relu(target_terms[:, :, None] + block_source[:, None, :])
        edge_scores = jnp.where(linked[None], edge_scores, -1e30)
        new_peak = jnp.maximum(running, jnp.max(edge_scores, axis=-1))
        edge_weights = jnp.where(linked[None], jnp.exp(edge_scores - new_peak[:, :, None]), 0.0)
        factor = jnp.exp(running - new_peak)
        denominator = denominator * factor + jnp.sum(edge_weights, axis=-1)
        update = jnp.einsum(
            "htb,bhd->htd",
            edge_weights.astype(jnp.bfloat16),
            block_values.reshape(span_rows, heads_here, head_width),
            preferred_element_type=jnp.float32,
        )
        accum = accum * factor[:, :, None] + update
        return ((new_peak, denominator, accum), None)

    initial = (
        jnp.full((heads_here, target_count), -1e30, jnp.float32),
        jnp.zeros((heads_here, target_count), jnp.float32),
        jnp.zeros((heads_here, target_count, head_width), jnp.float32),
    )
    carry = initial
    block_values = project(lax.all_gather(features, "node", axis=0, tiled=True))
    total_rows = block_values.shape[0]
    stride = math.gcd(total_rows, 1024)
    blocks = total_rows // stride
    block_source = head_terms(block_values, score_source)
    stacked = (
        block_values.reshape(blocks, stride, heads_here * head_width),
        block_source.reshape(heads_here, blocks, stride).transpose(1, 0, 2),
        stride * jnp.arange(blocks, dtype=jnp.int32),
    )
    carry, unused = lax.scan(absorb, carry, stacked)
    running, denominator, accum = carry
    heads_out = jax.nn.elu(accum / denominator[:, :, None]).astype(jnp.bfloat16)
    heads_out = heads_out.transpose(1, 0, 2).reshape(target_count, heads_here * head_width)
    partial_sum = jnp.dot(heads_out, out_weight, preferred_element_type=jnp.float32)
    result = lax.psum(partial_sum.astype(jnp.bfloat16), "head")
    return result


def solution(mesh):
    return jax.shard_map(
        per_device,
        mesh=mesh,
        in_specs=(
            P("node", None),
            P(None, "head"),
            P("head", None),
            P("head", None),
            P("head", None),
            P("node", None),
            P("node", None, None, None),
        ),
        out_specs=P("node", None),
        check_vma=False,
    )
```

profile of v0, /device:TPU:2, one launch (start us, length us, event | category | flops | bytes accessed | tf_op | source)
XLA Modules:
  0.0 1015.9 jit_solution(6120727612200111464)
XLA Ops:
  7.4 1.6 copy.9
  9.5 140.4 %all-gather.2.cloned.1.call-done = bf16[8192,128]{1,0:T(8,128)(2,1)} async-done(((bf16[128,128]{1,0:T(8,128)(2,1)}), bf16[8192,128]{1,0:T(8,128)(2,1)}) %all-gather.2.cloned.1.call-update) | async-done | bytes 2097168 | tf_op jit(solution)/shard_map/all_gather | solution.py:72
  149.8 2.3 convolution_convert_fusion
  152.1 1.2 multiply_reduce_fusion
  153.5 781.3 %while.17 = (s32[]{:T(128)}, f32[1,128]{1,0:T(1,128)S(1)}, f32[1,128]{1,0:T(1,128)S(1)}, f32[1,128,128]{2,1,0:T(8,128)S(1)}, s32[8]{0:T(128)S(1)}, /*index=5*/s3...) while((s32[]{:T(128)}, f32[1,128]{1,0:T(1,128)S(1)}, ...), condition=%wide.region_6.8_spmd.clone, body=%wide.region_3.7_spmd.clone.sunk | while | flops 37613440 | bytes 2482873 | solution.py:82
  157.0 40.4 %select_select_fusion.5 = s32[1024]{0:T(1024)S(1)} fusion(s32[]{:T(128)} %bitcast.403, s32[]{:T(128)} %bitcast.404, s32[]{:T(128)} %bitcast.405, s32[]{:T(128)} %bitcast.406, s32[]{:T(128)} %bitcast.407, s32[]{:T(128)} %bitcast.408, s32[]{:T(128)} %bitcast.409, s32[]{:T(128)} %bitcast.410, s32[]{:T(128)} %bitcast.411, s32[]{:T(128)} %bitcast.412, ...), kind=kLoop, calls=%fused_computation.49.clone.1 | loop fusion | flops 152576 | bytes 4356 | tf_op jit(solution)/shard_map/while/body/eval_jaxpr/jit(_take)/select_n | solution.py:42
  198.2 6.8 gather_fusion
  207.2 40.6 %select_select_fusion.4 = s32[1024]{0:T(1024)S(1)} fusion(s32[]{:T(128)} %bitcast.339, s32[]{:T(128)} %bitcast.340, s32[]{:T(128)} %bitcast.341, s32[]{:T(128)} %bitcast.342, s32[]{:T(128)} %bitcast.343, s32[]{:T(128)} %bitcast.344, s32[]{:T(128)} %bitcast.345, s32[]{:T(128)} %bitcast.346, s32[]{:T(128)} %bitcast.347, s32[]{:T(128)} %bitcast.348, ...), kind=kLoop, calls=%fused_computation.48.clone.1 | loop fusion | flops 152576 | bytes 4356 | tf_op jit(solution)/shard_map/while/body/eval_jaxpr/jit(_take)/select_n | solution.py:41
  248.6 0.7 fusion.83
  249.3 1.5 fusion.87
  254.7 40.4 %select_select_fusion.5 = s32[1024]{0:T(1024)S(1)} fusion(s32[]{:T(128)} %bitcast.403, s32[]{:T(128)} %bitcast.404, s32[]{:T(128)} %bitcast.405, s32[]{:T(128)} %bitcast.406, s32[]{:T(128)} %bitcast.407, s32[]{:T(128)} %bitcast.408, s32[]{:T(128)} %bitcast.409, s32[]{:T(128)} %bitcast.410, s32[]{:T(128)} %bitcast.411, s32[]{:T(128)} %bitcast.412, ...), kind=kLoop, calls=%fused_computation.49.clone.1 | loop fusion | flops 152576 | bytes 4356 | tf_op jit(solution)/shard_map/while/body/eval_jaxpr/jit(_take)/select_n | solution.py:42
  295.9 6.8 gather_fusion
  304.9 40.6 %select_select_fusion.4 = s32[1024]{0:T(1024)S(1)} fusion(s32[]{:T(128)} %bitcast.339, s32[]{:T(128)} %bitcast.340, s32[]{:T(128)} %bitcast.341, s32[]{:T(128)} %bitcast.342, s32[]{:T(128)} %bitcast.343, s32[]{:T(128)} %bitcast.344, s32[]{:T(128)} %bitcast.345, s32[]{:T(128)} %bitcast.346, s32[]{:T(128)} %bitcast.347, s32[]{:T(128)} %bitcast.348, ...), kind=kLoop, calls=%fused_computation.48.clone.1 | loop fusion | flops 152576 | bytes 4356 | tf_op jit(solution)/shard_map/while/body/eval_jaxpr/jit(_take)/select_n | solution.py:41
  346.2 0.7 fusion.83
  347.0 1.5 fusion.87
  352.3 40.4 %select_select_fusion.5 = s32[1024]{0:T(1024)S(1)} fusion(s32[]{:T(128)} %bitcast.403, s32[]{:T(128)} %bitcast.404, s32[]{:T(128)} %bitcast.405, s32[]{:T(128)} %bitcast.406, s32[]{:T(128)} %bitcast.407, s32[]{:T(128)} %bitcast.408, s32[]{:T(128)} %bitcast.409, s32[]{:T(128)} %bitcast.410, s32[]{:T(128)} %bitcast.411, s32[]{:T(128)} %bitcast.412, ...), kind=kLoop, calls=%fused_computation.49.clone.1 | loop fusion | flops 152576 | bytes 4356 | tf_op jit(solution)/shard_map/while/body/eval_jaxpr/jit(_take)/select_n | solution.py:42
  393.6 6.8 gather_fusion
  402.6 40.6 %select_select_fusion.4 = s32[1024]{0:T(1024)S(1)} fusion(s32[]{:T(128)} %bitcast.339, s32[]{:T(128)} %bitcast.340, s32[]{:T(128)} %bitcast.341, s32[]{:T(128)} %bitcast.342, s32[]{:T(128)} %bitcast.343, s32[]{:T(128)} %bitcast.344, s32[]{:T(128)} %bitcast.345, s32[]{:T(128)} %bitcast.346, s32[]{:T(128)} %bitcast.347, s32[]{:T(128)} %bitcast.348, ...), kind=kLoop, calls=%fused_computation.48.clone.1 | loop fusion | flops 152576 | bytes 4356 | tf_op jit(solution)/shard_map/while/body/eval_jaxpr/jit(_take)/select_n | solution.py:41
  443.9 0.7 fusion.83
  444.7 1.5 fusion.87
  450.0 40.4 %select_select_fusion.5 = s32[1024]{0:T(1024)S(1)} fusion(s32[]{:T(128)} %bitcast.403, s32[]{:T(128)} %bitcast.404, s32[]{:T(128)} %bitcast.405, s32[]{:T(128)} %bitcast.406, s32[]{:T(128)} %bitcast.407, s32[]{:T(128)} %bitcast.408, s32[]{:T(128)} %bitcast.409, s32[]{:T(128)} %bitcast.410, s32[]{:T(128)} %bitcast.411, s32[]{:T(128)} %bitcast.412, ...), kind=kLoop, calls=%fused_computation.49.clone.1 | loop fusion | flops 152576 | bytes 4356 | tf_op jit(solution)/shard_map/while/body/eval_jaxpr/jit(_take)/select_n | solution.py:42
  491.2 6.8 gather_fusion
  500.2 40.6 %select_select_fusion.4 = s32[1024]{0:T(1024)S(1)} fusion(s32[]{:T(128)} %bitcast.339, s32[]{:T(128)} %bitcast.340, s32[]{:T(128)} %bitcast.341, s32[]{:T(128)} %bitcast.342, s32[]{:T(128)} %bitcast.343, s32[]{:T(128)} %bitcast.344, s32[]{:T(128)} %bitcast.345, s32[]{:T(128)} %bitcast.346, s32[]{:T(128)} %bitcast.347, s32[]{:T(128)} %bitcast.348, ...), kind=kLoop, calls=%fused_computation.48.clone.1 | loop fusion | flops 152576 | bytes 4356 | tf_op jit(solution)/shard_map/while/body/eval_jaxpr/jit(_take)/select_n | solution.py:41
  541.6 0.7 fusion.83
  542.3 1.4 fusion.87
  547.7 40.4 %select_select_fusion.5 = s32[1024]{0:T(1024)S(1)} fusion(s32[]{:T(128)} %bitcast.403, s32[]{:T(128)} %bitcast.404, s32[]{:T(128)} %bitcast.405, s32[]{:T(128)} %bitcast.406, s32[]{:T(128)} %bitcast.407, s32[]{:T(128)} %bitcast.408, s32[]{:T(128)} %bitcast.409, s32[]{:T(128)} %bitcast.410, s32[]{:T(128)} %bitcast.411, s32[]{:T(128)} %bitcast.412, ...), kind=kLoop, calls=%fused_computation.49.clone.1 | loop fusion | flops 152576 | bytes 4356 | tf_op jit(solution)/shard_map/while/body/eval_jaxpr/jit(_take)/select_n | solution.py:42
  588.9 6.8 gather_fusion
  597.9 40.6 %select_select_fusion.4 = s32[1024]{0:T(1024)S(1)} fusion(s32[]{:T(128)} %bitcast.339, s32[]{:T(128)} %bitcast.340, s32[]{:T(128)} %bitcast.341, s32[]{:T(128)} %bitcast.342, s32[]{:T(128)} %bitcast.343, s32[]{:T(128)} %bitcast.344, s32[]{:T(128)} %bitcast.345, s32[]{:T(128)} %bitcast.346, s32[]{:T(128)} %bitcast.347, s32[]{:T(128)} %bitcast.348, ...), kind=kLoop, calls=%fused_computation.48.clone.1 | loop fusion | flops 152576 | bytes 4356 | tf_op jit(solution)/shard_map/while/body/eval_jaxpr/jit(_take)/select_n | solution.py:41
  639.2 0.7 fusion.83
  640.0 1.4 fusion.87
  645.3 40.4 %select_select_fusion.5 = s32[1024]{0:T(1024)S(1)} fusion(s32[]{:T(128)} %bitcast.403, s32[]{:T(128)} %bitcast.404, s32[]{:T(128)} %bitcast.405, s32[]{:T(128)} %bitcast.406, s32[]{:T(128)} %bitcast.407, s32[]{:T(128)} %bitcast.408, s32[]{:T(128)} %bitcast.409, s32[]{:T(128)} %bitcast.410, s32[]{:T(128)} %bitcast.411, s32[]{:T(128)} %bitcast.412, ...), kind=kLoop, calls=%fused_computation.49.clone.1 | loop fusion | flops 152576 | bytes 4356 | tf_op jit(solution)/shard_map/while/body/eval_jaxpr/jit(_take)/select_n | solution.py:42
  686.6 6.8 gather_fusion
  695.6 40.6 %select_select_fusion.4 = s32[1024]{0:T(1024)S(1)} fusion(s32[]{:T(128)} %bitcast.339, s32[]{:T(128)} %bitcast.340, s32[]{:T(128)} %bitcast.341, s32[]{:T(128)} %bitcast.342, s32[]{:T(128)} %bitcast.343, s32[]{:T(128)} %bitcast.344, s32[]{:T(128)} %bitcast.345, s32[]{:T(128)} %bitcast.346, s32[]{:T(128)} %bitcast.347, s32[]{:T(128)} %bitcast.348, ...), kind=kLoop, calls=%fused_computation.48.clone.1 | loop fusion | flops 152576 | bytes 4356 | tf_op jit(solution)/shard_map/while/body/eval_jaxpr/jit(_take)/select_n | solution.py:41
  736.9 0.7 fusion.83
  737.7 1.5 fusion.87
  743.0 40.4 %select_select_fusion.5 = s32[1024]{0:T(1024)S(1)} fusion(s32[]{:T(128)} %bitcast.403, s32[]{:T(128)} %bitcast.404, s32[]{:T(128)} %bitcast.405, s32[]{:T(128)} %bitcast.406, s32[]{:T(128)} %bitcast.407, s32[]{:T(128)} %bitcast.408, s32[]{:T(128)} %bitcast.409, s32[]{:T(128)} %bitcast.410, s32[]{:T(128)} %bitcast.411, s32[]{:T(128)} %bitcast.412, ...), kind=kLoop, calls=%fused_computation.49.clone.1 | loop fusion | flops 152576 | bytes 4356 | tf_op jit(solution)/shard_map/while/body/eval_jaxpr/jit(_take)/select_n | solution.py:42
  784.2 6.8 gather_fusion
  793.2 40.6 %select_select_fusion.4 = s32[1024]{0:T(1024)S(1)} fusion(s32[]{:T(128)} %bitcast.339, s32[]{:T(128)} %bitcast.340, s32[]{:T(128)} %bitcast.341, s32[]{:T(128)} %bitcast.342, s32[]{:T(128)} %bitcast.343, s32[]{:T(128)} %bitcast.344, s32[]{:T(128)} %bitcast.345, s32[]{:T(128)} %bitcast.346, s32[]{:T(128)} %bitcast.347, s32[]{:T(128)} %bitcast.348, ...), kind=kLoop, calls=%fused_computation.48.clone.1 | loop fusion | flops 152576 | bytes 4356 | tf_op jit(solution)/shard_map/while/body/eval_jaxpr/jit(_take)/select_n | solution.py:41
  834.6 0.7 fusion.83
  835.3 1.5 fusion.87
  840.7 40.4 %select_select_fusion.5 = s32[1024]{0:T(1024)S(1)} fusion(s32[]{:T(128)} %bitcast.403, s32[]{:T(128)} %bitcast.404, s32[]{:T(128)} %bitcast.405, s32[]{:T(128)} %bitcast.406, s32[]{:T(128)} %bitcast.407, s32[]{:T(128)} %bitcast.408, s32[]{:T(128)} %bitcast.409, s32[]{:T(128)} %bitcast.410, s32[]{:T(128)} %bitcast.411, s32[]{:T(128)} %bitcast.412, ...), kind=kLoop, calls=%fused_computation.49.clone.1 | loop fusion | flops 152576 | bytes 4356 | tf_op jit(solution)/shard_map/while/body/eval_jaxpr/jit(_take)/select_n | solution.py:42
  881.9 6.8 gather_fusion
  890.9 40.6 %select_select_fusion.4 = s32[1024]{0:T(1024)S(1)} fusion(s32[]{:T(128)} %bitcast.339, s32[]{:T(128)} %bitcast.340, s32[]{:T(128)} %bitcast.341, s32[]{:T(128)} %bitcast.342, s32[]{:T(128)} %bitcast.343, s32[]{:T(128)} %bitcast.344, s32[]{:T(128)} %bitcast.345, s32[]{:T(128)} %bitcast.346, s32[]{:T(128)} %bitcast.347, s32[]{:T(128)} %bitcast.348, ...), kind=kLoop, calls=%fused_computation.48.clone.1 | loop fusion | flops 152576 | bytes 4356 | tf_op jit(solution)/shard_map/while/body/eval_jaxpr/jit(_take)/select_n | solution.py:41
  932.2 0.7 fusion.83
  933.0 1.5 fusion.87
  934.8 0.9 convolution_convert_fusion.1
  935.7 71.9 %all-reduce.2.cloned.1.call-done = bf16[128,256]{1,0:T(8,128)(2,1)} async-done(((bf16[128,256]{1,0:T(8,128)(2,1)}), bf16[128,256]{1,0:T(8,128)(2,1)}) %all-reduce.2.cloned.1.call-update) | async-done | bytes 65552 | tf_op jit(solution)/shard_map/psum | solution.py:87
  1007.6 1.5 copy.26
  (186 shorter events, 61.4 us)
Async XLA Ops:
  6.5 928.3 %copy-start = (bf16[128,256]{1,0:T(8,128)(2,1)S(1)}, bf16[128,256]{1,0:T(8,128)(2,1)}, u32[]{:S(2)}) copy-start(bf16[128,256]{1,0:T(8,128)(2,1)} %param.15) | copy-start | bytes 196612
  6.5 2.4 copy-start.4
  6.5 2.4 copy-start.3
  6.5 2.5 copy-start.1
  6.5 2.8 copy-start.5
  6.5 143.3 %all-gather.2.cloned.1.call-start = ((), (), s32[]{:S(2)}) async-start(), calls=%async_computation | async-start | bytes 2129920 | tf_op jit(solution)/shard_map/all_gather | solution.py:72
  7.3 1000.3 %all-reduce.2.cloned.1.call-start = ((), (), s32[]{:S(2)}) async-start(), calls=%async_computation.1 | async-start | bytes 131072 | tf_op jit(solution)/shard_map/psum | solution.py:87
  9.5 142.7 %copy-start.6 = (f32[1,128]{1,0:T(1,128)S(1)}, f32[1,128]{1,0:T(1,128)}, u32[]{:S(2)}) copy-start(f32[1,128]{1,0:T(1,128)} %param.13) | copy-start | bytes 1540
  152.1 1.3 copy-start.2
Sparse Core Ops, SparseCore 0:
  11.7 138.0 all-gather.1
  935.8 71.6 all-reduce.1
where the time goes:
time: 1030 us; the launch traced here: 1020 us
  other arithmetic  670 us (65%)
  waiting for transfers between devices  213 us (21%)
  local copies, waits for them, and re-layouts  104 us (10%)
  matrix products  14.9 us (1%)
  between operations  13.5 us (1%)
    select_n x8, other arithmetic, absorb(): present_here = jnp.take(presence, column_tiles, axis=1)  325 us
    select_n x8, other arithmetic, absorb(): slot_here = jnp.take(slots, column_tiles, axis=1)  323 us
    all_gather x1, waiting for transfers between devices, per_device(): block_values = project(lax.all_gather(features, 'node', axis=0, tiled=True))  140 us
    psum x1, waiting for transfers between devices, per_device(): result = lax.psum(partial_sum.astype(jnp.bfloat16), 'head')  71.9 us
    gather x8, local copies, waits for them, and re-layouts, absorb(): tile_masks[tile_rows[:, None], slot_here, :, column_lanes[None, :]]  54.3 us
    gather x32, local copies, waits for them, and re-layouts, absorb(): slot_here = jnp.take(slots, column_tiles, axis=1)  23.1 us
  transfers between devices with their start and end apart: 2, of which 2 were waited for; matrix products, arithmetic and copies ran while one was open for 0% of the time, Pallas kernels for 0%

commit v1 on v0

--- a/solution.py
+++ b/solution.py
@@ -69,7 +69,16 @@
         jnp.zeros((heads_here, target_count, head_width), jnp.float32),
     )
     carry = initial
-    block_values = project(lax.all_gather(features, "node", axis=0, tiled=True))
+
+    def render_map(in_dim, which_axis, raw):
+        return jnp.concatenate(
+            jax.lax.all_to_all(
+                jnp.stack([raw] * jax.lax.psum(1, axis_name=which_axis), axis=0), which_axis, 0, 0
+            ),
+            axis=in_dim,
+        )
+
+    block_values = project(render_map(0, "node", features))
     total_rows = block_values.shape[0]
     stride = math.gcd(total_rows, 1024)
     blocks = total_rows // stride

time: 1030 us -> 957 us (0.929)
  waiting for transfers between devices: 213 us -> 127 us
  starting transfers between devices: 0.08 us -> 19.2 us
    all_gather x1 -> x0, waiting for transfers between devices: 140 us -> none  [per_device(): block_values = project(lax.all_gather(features, 'node', axis=0, tiled=True))]
    all_to_all x0 -> x1, waiting for transfers between devices: none -> 46.2 us  [render_map(): jax.lax.all_to_all(jnp.stack([raw] * jax.lax.psum(1, axis_name=which_axis...]
    all_to_all x0 -> x1, starting transfers between devices: none -> 19.1 us  [render_map(): jax.lax.all_to_all(jnp.stack([raw] * jax.lax.psum(1, axis_name=which_axis...]
where the time goes in v1:
time: 957 us; the launch traced here: 947 us
  other arithmetic  667 us (70%)
  waiting for transfers between devices  127 us (13%)
  local copies, waits for them, and re-layouts  105 us (11%)
  starting transfers between devices  19.2 us (2%)
  between operations  13.6 us (1%)
  matrix products  13.3 us (1%)
    select_n x8, other arithmetic, absorb(): present_here = jnp.take(presence, column_tiles, axis=1)  325 us
    select_n x8, other arithmetic, absorb(): slot_here = jnp.take(slots, column_tiles, axis=1)  323 us
    psum x1, waiting for transfers between devices, per_device(): result = lax.psum(partial_sum.astype(jnp.bfloat16), 'head')  81 us
    gather x8, local copies, waits for them, and re-layouts, absorb(): tile_masks[tile_rows[:, None], slot_here, :, column_lanes[None, :]]  54.3 us
    all_to_all x1, waiting for transfers between devices, render_map(): jax.lax.all_to_all(jnp.stack([raw] * jax.lax.psum(1, axis_name=which_axis...  46.2 us
    gather x32, local copies, waits for them, and re-layouts, absorb(): slot_here = jnp.take(slots, column_tiles, axis=1)  23.1 us
  transfers between devices with their start and end apart: 2, of which 2 were waited for; matrix products, arithmetic and copies ran while one was open for 0% of the time, Pallas kernels for 0%

profile of v1, /device:TPU:2, one launch (start us, length us, event | category | flops | bytes accessed | tf_op | source)
XLA Modules:
  0.0 947.0 jit_solution(8354182267524966070)
XLA Ops:
  6.5 2.6 stack.2
  9.2 19.1 %all-to-all-start = ((bf16[64,128,128]{2,1,0:T(8,128)(2,1)}), bf16[64,128,128]{2,1,0:T(8,128)(2,1)S(1)}, u32[]{:S(2)}, u32[]{:S(2)}) async-start(bf16[64,128,128]{2,1,0:T(8,128)(2,1)} %stack.2), calls=%async_computation | async-start | bytes 4194304 | tf_op jit(solution)/shard_map/all_to_all | solution.py:75
  28.4 1.6 copy.9
  30.5 46.2 %all-to-all-done = bf16[64,128,128]{2,1,0:T(8,128)(2,1)S(1)} async-done(((bf16[64,128,128]{2,1,0:T(8,128)(2,1)}), bf16[64,128,128]{2,1,0:T(8,128)(2,1)S(1)}, u32[]{:S(2)}, u32[]{:S(2)}) %all-to-all-start) | async-done | bytes 2097184 | tf_op jit(solution)/shard_map/all_to_all | solution.py:75
  77.4 1.2 multiply_reduce_fusion
  78.7 778.0 %while.17 = (s32[]{:T(128)}, f32[1,128]{1,0:T(1,128)S(1)}, f32[1,128]{1,0:T(1,128)S(1)}, f32[1,128,128]{2,1,0:T(8,128)S(1)}, s32[8]{0:T(128)S(1)}, /*index=5*/s3...) while((s32[]{:T(128)}, f32[1,128]{1,0:T(1,128)S(1)}, ...), condition=%wide.region_6.8_spmd.clone, body=%wide.region_3.7_spmd.clone.sunk | while | flops 37613440 | bytes 2482873 | solution.py:91
  82.2 40.3 %select_select_fusion.5 = s32[1024]{0:T(1024)S(1)} fusion(s32[]{:T(128)} %bitcast.404, s32[]{:T(128)} %bitcast.405, s32[]{:T(128)} %bitcast.406, s32[]{:T(128)} %bitcast.407, s32[]{:T(128)} %bitcast.408, s32[]{:T(128)} %bitcast.409, s32[]{:T(128)} %bitcast.410, s32[]{:T(128)} %bitcast.411, s32[]{:T(128)} %bitcast.412, s32[]{:T(128)} %bitcast.413, ...), kind=kLoop, calls=%fused_computation.49.clone.1 | loop fusion | flops 152576 | bytes 4356 | tf_op jit(solution)/shard_map/while/body/eval_jaxpr/jit(_take)/select_n | solution.py:42
  123.2 6.8 gather_fusion
  132.2 40.6 %select_select_fusion.4 = s32[1024]{0:T(1024)S(1)} fusion(s32[]{:T(128)} %bitcast.340, s32[]{:T(128)} %bitcast.341, s32[]{:T(128)} %bitcast.342, s32[]{:T(128)} %bitcast.343, s32[]{:T(128)} %bitcast.344, s32[]{:T(128)} %bitcast.345, s32[]{:T(128)} %bitcast.346, s32[]{:T(128)} %bitcast.347, s32[]{:T(128)} %bitcast.348, s32[]{:T(128)} %bitcast.349, ...), kind=kLoop, calls=%fused_computation.48.clone.1 | loop fusion | flops 152576 | bytes 4356 | tf_op jit(solution)/shard_map/while/body/eval_jaxpr/jit(_take)/select_n | solution.py:41
  173.4 0.7 fusion.83
  174.2 1.5 fusion.87
  179.5 40.3 %select_select_fusion.5 = s32[1024]{0:T(1024)S(1)} fusion(s32[]{:T(128)} %bitcast.404, s32[]{:T(128)} %bitcast.405, s32[]{:T(128)} %bitcast.406, s32[]{:T(128)} %bitcast.407, s32[]{:T(128)} %bitcast.408, s32[]{:T(128)} %bitcast.409, s32[]{:T(128)} %bitcast.410, s32[]{:T(128)} %bitcast.411, s32[]{:T(128)} %bitcast.412, s32[]{:T(128)} %bitcast.413, ...), kind=kLoop, calls=%fused_computation.49.clone.1 | loop fusion | flops 152576 | bytes 4356 | tf_op jit(solution)/shard_map/while/body/eval_jaxpr/jit(_take)/select_n | solution.py:42
  220.5 6.8 gather_fusion
  229.4 40.6 %select_select_fusion.4 = s32[1024]{0:T(1024)S(1)} fusion(s32[]{:T(128)} %bitcast.340, s32[]{:T(128)} %bitcast.341, s32[]{:T(128)} %bitcast.342, s32[]{:T(128)} %bitcast.343, s32[]{:T(128)} %bitcast.344, s32[]{:T(128)} %bitcast.345, s32[]{:T(128)} %bitcast.346, s32[]{:T(128)} %bitcast.347, s32[]{:T(128)} %bitcast.348, s32[]{:T(128)} %bitcast.349, ...), kind=kLoop, calls=%fused_computation.48.clone.1 | loop fusion | flops 152576 | bytes 4356 | tf_op jit(solution)/shard_map/while/body/eval_jaxpr/jit(_take)/select_n | solution.py:41
  270.7 0.7 fusion.83
  271.5 1.5 fusion.87
  276.7 40.3 %select_select_fusion.5 = s32[1024]{0:T(1024)S(1)} fusion(s32[]{:T(128)} %bitcast.404, s32[]{:T(128)} %bitcast.405, s32[]{:T(128)} %bitcast.406, s32[]{:T(128)} %bitcast.407, s32[]{:T(128)} %bitcast.408, s32[]{:T(128)} %bitcast.409, s32[]{:T(128)} %bitcast.410, s32[]{:T(128)} %bitcast.411, s32[]{:T(128)} %bitcast.412, s32[]{:T(128)} %bitcast.413, ...), kind=kLoop, calls=%fused_computation.49.clone.1 | loop fusion | flops 152576 | bytes 4356 | tf_op jit(solution)/shard_map/while/body/eval_jaxpr/jit(_take)/select_n | solution.py:42
  317.7 6.8 gather_fusion
  326.7 40.6 %select_select_fusion.4 = s32[1024]{0:T(1024)S(1)} fusion(s32[]{:T(128)} %bitcast.340, s32[]{:T(128)} %bitcast.341, s32[]{:T(128)} %bitcast.342, s32[]{:T(128)} %bitcast.343, s32[]{:T(128)} %bitcast.344, s32[]{:T(128)} %bitcast.345, s32[]{:T(128)} %bitcast.346, s32[]{:T(128)} %bitcast.347, s32[]{:T(128)} %bitcast.348, s32[]{:T(128)} %bitcast.349, ...), kind=kLoop, calls=%fused_computation.48.clone.1 | loop fusion | flops 152576 | bytes 4356 | tf_op jit(solution)/shard_map/while/body/eval_jaxpr/jit(_take)/select_n | solution.py:41
  367.9 0.7 fusion.83
  368.7 1.5 fusion.87
  374.0 40.3 %select_select_fusion.5 = s32[1024]{0:T(1024)S(1)} fusion(s32[]{:T(128)} %bitcast.404, s32[]{:T(128)} %bitcast.405, s32[]{:T(128)} %bitcast.406, s32[]{:T(128)} %bitcast.407, s32[]{:T(128)} %bitcast.408, s32[]{:T(128)} %bitcast.409, s32[]{:T(128)} %bitcast.410, s32[]{:T(128)} %bitcast.411, s32[]{:T(128)} %bitcast.412, s32[]{:T(128)} %bitcast.413, ...), kind=kLoop, calls=%fused_computation.49.clone.1 | loop fusion | flops 152576 | bytes 4356 | tf_op jit(solution)/shard_map/while/body/eval_jaxpr/jit(_take)/select_n | solution.py:42
  415.0 6.8 gather_fusion
  424.0 40.6 %select_select_fusion.4 = s32[1024]{0:T(1024)S(1)} fusion(s32[]{:T(128)} %bitcast.340, s32[]{:T(128)} %bitcast.341, s32[]{:T(128)} %bitcast.342, s32[]{:T(128)} %bitcast.343, s32[]{:T(128)} %bitcast.344, s32[]{:T(128)} %bitcast.345, s32[]{:T(128)} %bitcast.346, s32[]{:T(128)} %bitcast.347, s32[]{:T(128)} %bitcast.348, s32[]{:T(128)} %bitcast.349, ...), kind=kLoop, calls=%fused_computation.48.clone.1 | loop fusion | flops 152576 | bytes 4356 | tf_op jit(solution)/shard_map/while/body/eval_jaxpr/jit(_take)/select_n | solution.py:41
  465.2 0.7 fusion.83
  466.0 1.5 fusion.87
  471.2 40.3 %select_select_fusion.5 = s32[1024]{0:T(1024)S(1)} fusion(s32[]{:T(128)} %bitcast.404, s32[]{:T(128)} %bitcast.405, s32[]{:T(128)} %bitcast.406, s32[]{:T(128)} %bitcast.407, s32[]{:T(128)} %bitcast.408, s32[]{:T(128)} %bitcast.409, s32[]{:T(128)} %bitcast.410, s32[]{:T(128)} %bitcast.411, s32[]{:T(128)} %bitcast.412, s32[]{:T(128)} %bitcast.413, ...), kind=kLoop, calls=%fused_computation.49.clone.1 | loop fusion | flops 152576 | bytes 4356 | tf_op jit(solution)/shard_map/while/body/eval_jaxpr/jit(_take)/select_n | solution.py:42
  512.2 6.8 gather_fusion
  521.2 40.6 %select_select_fusion.4 = s32[1024]{0:T(1024)S(1)} fusion(s32[]{:T(128)} %bitcast.340, s32[]{:T(128)} %bitcast.341, s32[]{:T(128)} %bitcast.342, s32[]{:T(128)} %bitcast.343, s32[]{:T(128)} %bitcast.344, s32[]{:T(128)} %bitcast.345, s32[]{:T(128)} %bitcast.346, s32[]{:T(128)} %bitcast.347, s32[]{:T(128)} %bitcast.348, s32[]{:T(128)} %bitcast.349, ...), kind=kLoop, calls=%fused_computation.48.clone.1 | loop fusion | flops 152576 | bytes 4356 | tf_op jit(solution)/shard_map/while/body/eval_jaxpr/jit(_take)/select_n | solution.py:41
  562.5 0.7 fusion.83
  563.2 1.5 fusion.87
  568.5 40.3 %select_select_fusion.5 = s32[1024]{0:T(1024)S(1)} fusion(s32[]{:T(128)} %bitcast.404, s32[]{:T(128)} %bitcast.405, s32[]{:T(128)} %bitcast.406, s32[]{:T(128)} %bitcast.407, s32[]{:T(128)} %bitcast.408, s32[]{:T(128)} %bitcast.409, s32[]{:T(128)} %bitcast.410, s32[]{:T(128)} %bitcast.411, s32[]{:T(128)} %bitcast.412, s32[]{:T(128)} %bitcast.413, ...), kind=kLoop, calls=%fused_computation.49.clone.1 | loop fusion | flops 152576 | bytes 4356 | tf_op jit(solution)/shard_map/while/body/eval_jaxpr/jit(_take)/select_n | solution.py:42
  609.5 6.8 gather_fusion
  618.5 40.6 %select_select_fusion.4 = s32[1024]{0:T(1024)S(1)} fusion(s32[]{:T(128)} %bitcast.340, s32[]{:T(128)} %bitcast.341, s32[]{:T(128)} %bitcast.342, s32[]{:T(128)} %bitcast.343, s32[]{:T(128)} %bitcast.344, s32[]{:T(128)} %bitcast.345, s32[]{:T(128)} %bitcast.346, s32[]{:T(128)} %bitcast.347, s32[]{:T(128)} %bitcast.348, s32[]{:T(128)} %bitcast.349, ...), kind=kLoop, calls=%fused_computation.48.clone.1 | loop fusion | flops 152576 | bytes 4356 | tf_op jit(solution)/shard_map/while/body/eval_jaxpr/jit(_take)/select_n | solution.py:41
  659.7 0.7 fusion.83
  660.5 1.4 fusion.87
  665.8 40.3 %select_select_fusion.5 = s32[1024]{0:T(1024)S(1)} fusion(s32[]{:T(128)} %bitcast.404, s32[]{:T(128)} %bitcast.405, s32[]{:T(128)} %bitcast.406, s32[]{:T(128)} %bitcast.407, s32[]{:T(128)} %bitcast.408, s32[]{:T(128)} %bitcast.409, s32[]{:T(128)} %bitcast.410, s32[]{:T(128)} %bitcast.411, s32[]{:T(128)} %bitcast.412, s32[]{:T(128)} %bitcast.413, ...), kind=kLoop, calls=%fused_computation.49.clone.1 | loop fusion | flops 152576 | bytes 4356 | tf_op jit(solution)/shard_map/while/body/eval_jaxpr/jit(_take)/select_n | solution.py:42
  706.8 6.8 gather_fusion
  715.7 40.6 %select_select_fusion.4 = s32[1024]{0:T(1024)S(1)} fusion(s32[]{:T(128)} %bitcast.340, s32[]{:T(128)} %bitcast.341, s32[]{:T(128)} %bitcast.342, s32[]{:T(128)} %bitcast.343, s32[]{:T(128)} %bitcast.344, s32[]{:T(128)} %bitcast.345, s32[]{:T(128)} %bitcast.346, s32[]{:T(128)} %bitcast.347, s32[]{:T(128)} %bitcast.348, s32[]{:T(128)} %bitcast.349, ...), kind=kLoop, calls=%fused_computation.48.clone.1 | loop fusion | flops 152576 | bytes 4356 | tf_op jit(solution)/shard_map/while/body/eval_jaxpr/jit(_take)/select_n | solution.py:41
  757.0 0.7 fusion.83
  757.7 1.5 fusion.87
  763.0 40.3 %select_select_fusion.5 = s32[1024]{0:T(1024)S(1)} fusion(s32[]{:T(128)} %bitcast.404, s32[]{:T(128)} %bitcast.405, s32[]{:T(128)} %bitcast.406, s32[]{:T(128)} %bitcast.407, s32[]{:T(128)} %bitcast.408, s32[]{:T(128)} %bitcast.409, s32[]{:T(128)} %bitcast.410, s32[]{:T(128)} %bitcast.411, s32[]{:T(128)} %bitcast.412, s32[]{:T(128)} %bitcast.413, ...), kind=kLoop, calls=%fused_computation.49.clone.1 | loop fusion | flops 152576 | bytes 4356 | tf_op jit(solution)/shard_map/while/body/eval_jaxpr/jit(_take)/select_n | solution.py:42
  804.0 6.8 gather_fusion
  813.0 40.6 %select_select_fusion.4 = s32[1024]{0:T(1024)S(1)} fusion(s32[]{:T(128)} %bitcast.340, s32[]{:T(128)} %bitcast.341, s32[]{:T(128)} %bitcast.342, s32[]{:T(128)} %bitcast.343, s32[]{:T(128)} %bitcast.344, s32[]{:T(128)} %bitcast.345, s32[]{:T(128)} %bitcast.346, s32[]{:T(128)} %bitcast.347, s32[]{:T(128)} %bitcast.348, s32[]{:T(128)} %bitcast.349, ...), kind=kLoop, calls=%fused_computation.48.clone.1 | loop fusion | flops 152576 | bytes 4356 | tf_op jit(solution)/shard_map/while/body/eval_jaxpr/jit(_take)/select_n | solution.py:41
  855.0 1.4 fusion.87
  856.8 0.9 convolution_convert_fusion.1
  857.7 81.0 %all-reduce.2.cloned.1.call-done = bf16[128,256]{1,0:T(8,128)(2,1)} async-done(((bf16[128,256]{1,0:T(8,128)(2,1)}), bf16[128,256]{1,0:T(8,128)(2,1)}) %all-reduce.2.cloned.1.call-update) | async-done | bytes 65552 | tf_op jit(solution)/shard_map/psum | solution.py:96
  938.7 1.5 copy.26
  (186 shorter events, 59.6 us)
Async XLA Ops:
  6.5 850.2 %copy-start = (bf16[128,256]{1,0:T(8,128)(2,1)S(1)}, bf16[128,256]{1,0:T(8,128)(2,1)}, u32[]{:S(2)}) copy-start(bf16[128,256]{1,0:T(8,128)(2,1)} %param.15) | copy-start | bytes 196612
  9.2 67.5 %all-to-all-start = ((bf16[64,128,128]{2,1,0:T(8,128)(2,1)}), bf16[64,128,128]{2,1,0:T(8,128)(2,1)S(1)}, u32[]{:S(2)}, u32[]{:S(2)}) async-start(bf16[64,128,128]{2,1,0:T(8,128)(2,1)} %stack.2), calls=%async_computation | async-start | bytes 4194304 | tf_op jit(solution)/shard_map/all_to_all | solution.py:75
  28.3 1.7 copy-start.3
  28.3 1.7 copy-start.4
  28.3 1.8 copy-start.1
  28.3 2.1 copy-start.5
  28.3 910.3 %all-reduce.2.cloned.1.call-start = ((), (), s32[]{:S(2)}) async-start(), calls=%async_computation.1 | async-start | bytes 131072 | tf_op jit(solution)/shard_map/psum | solution.py:96
  76.7 0.7 copy-start.6
  77.4 1.3 copy-start.2
Sparse Core Ops, SparseCore 0:
  857.8 80.8 all-reduce.1
